TPU v7x, 512 devices: a whole 4x4x16 slice. The times are simulated.
512 devices in a mesh: clip: 4 (over x), tx: 16 (over z_lo, core), ty: 8 (over z_hi, y).
Axes of the slice: x: 4, y: 4, z: 16 (z_hi: 2, z_lo: 8; z = z_hi * 8 + z_lo), core: 2. Of those that a mesh axis runs over, the one named last changes fastest.
Arguments:
- query_states: bfloat16 [512, 128, 1152], P(('clip', 'tx', 'ty')), parts along dimension 0, may hold values from -64 to 64
- key_states: bfloat16 [512, 128, 1152], P(('clip', 'tx', 'ty')), parts along dimension 0, may hold values from -24 to 24
- value_states: bfloat16 [512, 128, 1152], P(('clip', 'tx', 'ty')), parts along dimension 0, may hold values from -6 to 6
- grad_output: bfloat16 [512, 128, 1152], P(('clip', 'tx', 'ty')), parts along dimension 0, may hold values from -6 to 6
- branch_gate: float32 [4608], P('clip'), parts along dimension 0, may hold values from 0.1 to 1.9
- out_weight: bfloat16 [1152, 1152], P('tx'), may hold values from -0.1875 to 0.1875
Outputs:
- query_grad: bfloat16 [512, 128, 1152], P(('clip', 'tx', 'ty')), parts along dimension 0
- key_grad: bfloat16 [512, 128, 1152], P(('clip', 'tx', 'ty')), parts along dimension 0
- value_grad: bfloat16 [512, 128, 1152], P(('clip', 'tx', 'ty')), parts along dimension 0
- gate_grad: float32 [4608], P('clip'), parts along dimension 0
There are 4 independent parts, one for each index of `clip`. A program takes and returns all parts, laid end to end along the dimension named above; an argument that names none is the same for every part. Nothing has to cross between parts.
All inputs are finite; a program needn't handle non-finite values.
Results may differ from a plain program's by a relative error of at most 0.025.
Values may be sent and summed in bfloat16 or wider, within the bound.
No kernel may reach another device: no remote copies, remote signals or barrier semaphores. Data moves between devices by JAX's collectives and lax.ppermute only.
A program may use at most 64 MiB of HBM per device.

v0:
```python
import jax
import jax.numpy as jnp
from jax import lax
from jax.sharding import Mesh
from jax.sharding import PartitionSpec as P

HEAD_DIM = 72
TX = ("tx_0", "tx_1")
TY = ("ty_0", "ty_1")
TX_TY = ("tx_0", "tx_1", "ty_0", "ty_1")
CLIP_TX_TY = ("clip", "tx_0", "tx_1", "ty_0", "ty_1")


def shortened(x):

    def short(part):
        return part.astype(jnp.bfloat16) if part.dtype == jnp.float32 else part

    return jax.tree.map(short, x)


def over_axes(x, axes):
    for axis in axes:
        x = lax.psum(x, axis)
    return x


def attend_block(queries, keys_in, values_in, grads_in):
    frames, block_pos, block_width = queries.shape
    heads_here = block_width // HEAD_DIM
    shape4 = (frames, block_pos, heads_here, HEAD_DIM)
    q_four = queries.reshape(shape4)
    k_four = keys_in.reshape(shape4)
    v_four = values_in.reshape(shape4)
    g_four = grads_in.reshape(shape4)
    factor = HEAD_DIM ** (-0.5)
    scores = (
        jnp.einsum("fphd,gphd->phfg", q_four, k_four, preferred_element_type=jnp.float32) * factor
    )
    peak = jnp.max(scores, axis=-1, keepdims=True)
    expon = jnp.exp(scores - peak)
    probs = expon / jnp.sum(expon, axis=-1, keepdims=True)
    probs_b = probs.astype(jnp.bfloat16)
    attn_out = jnp.einsum(
        "phfg,gphd->fphd", probs_b, v_four, preferred_element_type=jnp.float32
    ).astype(jnp.bfloat16)
    value_grad = jnp.einsum(
        "phfg,fphd->gphd", probs_b, g_four, preferred_element_type=jnp.float32
    ).astype(jnp.bfloat16)
    dprobs = jnp.einsum("fphd,gphd->phfg", g_four, v_four, preferred_element_type=jnp.float32)
    delta = jnp.sum(g_four.astype(jnp.float32) * attn_out.astype(jnp.float32), axis=-1)
    delta = jnp.transpose(delta, (1, 2, 0))[..., None]
    dscores = (probs * (dprobs - delta) * factor).astype(jnp.bfloat16)
    query_grad = jnp.einsum(
        "phfg,gphd->fphd", dscores, k_four, preferred_element_type=jnp.float32
    ).astype(jnp.bfloat16)
    key_grad = jnp.einsum(
        "phfg,fphd->gphd", dscores, q_four, preferred_element_type=jnp.float32
    ).astype(jnp.bfloat16)
    flat = (frames, block_pos, block_width)
    return (
        query_grad.reshape(flat),
        key_grad.reshape(flat),
        value_grad.reshape(flat),
        attn_out.reshape(flat),
    )


def split_for_direct(array, across_x, across_y):
    positions, width = array.shape
    pieces = array.reshape(across_y, positions // across_y, across_x, width // across_x)
    pieces = jnp.transpose(pieces, (2, 0, 1, 3))
    return pieces.reshape(1, across_x * across_y, positions // across_y, width // across_x)


def join_from_direct(array, across_x, across_y):
    block_pos, block_width = (array.shape[2], array.shape[3])
    pieces = array.reshape(across_x, across_y, block_pos, block_width)
    pieces = jnp.transpose(pieces, (1, 2, 0, 3))
    return pieces.reshape(1, across_y * block_pos, across_x * block_width)


def per_device(query_states, key_states, value_states, grad_output, branch_gate, out_weight):
    across_x = lax.axis_size(TX)
    across_y = lax.axis_size(TY)
    devices_here = across_x * across_y
    positions = grad_output.shape[1]
    width = grad_output.shape[2]
    block_pos = positions // across_y
    block_width = width // across_x
    grad_rows = grad_output[0]
    gated = (grad_rows.astype(jnp.float32) * branch_gate).astype(jnp.bfloat16)
    full_weight = lax.all_gather(out_weight, TX, axis=0, tiled=True)
    d_attn = lax.dot_general(
        gated, full_weight, (((1,), (1,)), ((), ())), preferred_element_type=jnp.float32
    )
    d_attn = d_attn.astype(jnp.bfloat16)
    sources = (query_states[0], key_states[0], value_states[0], d_attn)
    prepared = tuple((split_for_direct(arr, across_x, across_y) for arr in sources))
    moved = jax.tree.map(
        lambda part, own: part.astype(own.dtype),
        lax.all_to_all(shortened(prepared), TX_TY, split_axis=1, concat_axis=0, tiled=True),
        prepared,
    )
    moved = tuple((arr.reshape(devices_here, block_pos, block_width) for arr in moved))
    results = attend_block(moved[0], moved[1], moved[2], moved[3])
    outgoing = tuple((arr.reshape(devices_here, 1, block_pos, block_width) for arr in results))
    returned = jax.tree.map(
        lambda part, own: part.astype(own.dtype),
        lax.all_to_all(shortened(outgoing), TX_TY, split_axis=0, concat_axis=1, tiled=True),
        outgoing,
    )
    returned = tuple((join_from_direct(arr, across_x, across_y) for arr in returned))
    query_grad, key_grad, value_grad, attn_frame = returned
    attn_rows = attn_frame[0]
    branch_out = jnp.dot(attn_rows, full_weight, preferred_element_type=jnp.float32)
    local_terms = jnp.sum(grad_rows.astype(jnp.float32) * branch_out, axis=0)
    gate_grad = over_axes(local_terms, TX_TY)
    return (query_grad, key_grad, value_grad, gate_grad)


def solution(mesh):
    split = Mesh(
        mesh.devices.reshape(mesh.shape["clip"], 8, 2, 2, 4),
        ("clip", "tx_0", "tx_1", "ty_0", "ty_1"),
    )
    placed = (
        P(CLIP_TX_TY, None, None),
        P(CLIP_TX_TY, None, None),
        P(CLIP_TX_TY, None, None),
        P(CLIP_TX_TY, None, None),
        P("clip"),
        P(TX, None),
    )
    return jax.shard_map(
        per_device,
        mesh=split,
        in_specs=placed,
        out_specs=(
            P(CLIP_TX_TY, None, None),
            P(CLIP_TX_TY, None, None),
            P(CLIP_TX_TY, None, None),
            P("clip"),
        ),
        check_vma=False,
    )
```

profile of v0, /device:TPU:6, one launch (start us, length us, event | category | flops | bytes accessed | tf_op | source)
XLA Modules:
  0.0 446.0 jit_solution(15969806378032638530)
XLA Ops:
  10.8 20.0 %all-to-all-start = ((bf16[1,128,16,72]{3,2,0,1:T(8,128)(2,1)}), bf16[1,128,16,72]{3,2,0,1:T(8,128)(2,1)S(1)}, u32[]{:S(2)}, u32[]{:S(2)}) async-start(bf16[1,128,16,72]{3,2,0,1:T(8,128)(2,1)} %bitcast.2), calls=%async_computation | async-start | bytes 1048576 | tf_op jit(solution)/shard_map/all_to_all | solution.py:102
  32.6 33.7 %all-to-all-done = bf16[1,128,16,72]{3,2,0,1:T(8,128)(2,1)S(1)} async-done(((bf16[1,128,16,72]{3,2,0,1:T(8,128)(2,1)}), bf16[1,128,16,72]{3,2,0,1:T(8,128)(2,1)S(1)}, u32[]{:S(2)}, u32[]{:S(2)}) %all-to-all-start) | async-done | bytes 294944 | tf_op jit(solution)/shard_map/all_to_all | solution.py:102
  66.3 9.5 %all-to-all-start.1 = ((bf16[1,128,16,72]{3,2,0,1:T(8,128)(2,1)}), bf16[1,128,16,72]{3,2,0,1:T(8,128)(2,1)S(1)}, u32[]{:S(2)}, u32[]{:S(2)}) async-start(bf16[1,128,16,72]{3,2,0,1:T(8,128)(2,1)} %bitcast.6), calls=%async_computation.1 | async-start | bytes 1048576 | tf_op jit(solution)/shard_map/all_to_all | solution.py:102
  75.9 68.5 %all-gather.2.cloned.1.call-done = bf16[1152,1152]{1,0:T(8,128)(2,1)} async-done(((bf16[72,1152]{1,0:T(8,128)(2,1)}), bf16[1152,1152]{1,0:T(8,128)(2,1)}) %all-gather.2.cloned.1.call-update) | async-done | bytes 2654224 | tf_op jit(solution)/shard_map/all_gather | solution.py:93
  144.4 2.7 convolution_convert_fusion
  149.0 12.0 %all-to-all-start.2 = ((bf16[1,128,16,72]{3,2,0,1:T(8,128)(2,1)}), bf16[1,128,16,72]{3,2,0,1:T(8,128)(2,1)S(1)}, u32[]{:S(2)}, u32[]{:S(2)}) async-start(bf16[1,128,16,72]{3,2,0,1:T(8,128)(2,1)} %bitcast.11), calls=%async_computation.2 | async-start | bytes 1048576 | tf_op jit(solution)/shard_map/all_to_all | solution.py:102
  162.9 28.8 %all-to-all-done.2 = bf16[1,128,16,72]{3,2,0,1:T(8,128)(2,1)S(1)} async-done(((bf16[1,128,16,72]{3,2,0,1:T(8,128)(2,1)}), bf16[1,128,16,72]{3,2,0,1:T(8,128)(2,1)S(1)}, u32[]{:S(2)}, u32[]{:S(2)}) %all-to-all-start.2) | async-done | bytes 294944 | tf_op jit(solution)/shard_map/all_to_all | solution.py:102
  191.7 9.7 %all-to-all-start.3 = ((bf16[1,128,16,72]{3,2,0,1:T(8,128)(2,1)}), bf16[1,128,16,72]{3,2,0,1:T(8,128)(2,1)S(1)}, u32[]{:S(2)}, u32[]{:S(2)}) async-start(bf16[1,128,16,72]{3,2,0,1:T(8,128)(2,1)} %bitcast.15), calls=%async_computation.3 | async-start | bytes 1048576 | tf_op jit(solution)/shard_map/all_to_all | solution.py:102
  207.2 24.7 %all-to-all-done.3 = bf16[1,128,16,72]{3,2,0,1:T(8,128)(2,1)S(1)} async-done(((bf16[1,128,16,72]{3,2,0,1:T(8,128)(2,1)}), bf16[1,128,16,72]{3,2,0,1:T(8,128)(2,1)S(1)}, u32[]{:S(2)}, u32[]{:S(2)}) %all-to-all-start.3) | async-done | bytes 294944 | tf_op jit(solution)/shard_map/all_to_all | solution.py:102
  231.8 9.5 %all-to-all-start.6 = ((bf16[128,1,16,72]{3,2,1,0:T(8,128)(2,1)}), bf16[128,1,16,72]{3,2,1,0:T(8,128)(2,1)S(1)}, u32[]{:S(2)}, u32[]{:S(2)}) async-start(bf16[128,1,16,72]{3,2,1,0:T(8,128)(2,1)} %copy.83), calls=%async_computation.6 | async-start | bytes 1048576 | tf_op jit(solution)/shard_map/all_to_all | solution.py:110
  244.7 27.3 %all-to-all-done.6 = bf16[128,1,16,72]{3,2,1,0:T(8,128)(2,1)S(1)} async-done(((bf16[128,1,16,72]{3,2,1,0:T(8,128)(2,1)}), bf16[128,1,16,72]{3,2,1,0:T(8,128)(2,1)S(1)}, u32[]{:S(2)}, u32[]{:S(2)}) %all-to-all-start.6) | async-done | bytes 294944 | tf_op jit(solution)/shard_map/all_to_all | solution.py:110
  272.0 9.5 %all-to-all-start.7 = ((bf16[128,1,16,72]{3,2,1,0:T(8,128)(2,1)}), bf16[128,1,16,72]{3,2,1,0:T(8,128)(2,1)S(1)}, u32[]{:S(2)}, u32[]{:S(2)}) async-start(bf16[128,1,16,72]{3,2,1,0:T(8,128)(2,1)} %copy.85), calls=%async_computation.7 | async-start | bytes 1048576 | tf_op jit(solution)/shard_map/all_to_all | solution.py:110
  284.8 27.4 %all-to-all-done.7 = bf16[128,1,16,72]{3,2,1,0:T(8,128)(2,1)S(1)} async-done(((bf16[128,1,16,72]{3,2,1,0:T(8,128)(2,1)}), bf16[128,1,16,72]{3,2,1,0:T(8,128)(2,1)S(1)}, u32[]{:S(2)}, u32[]{:S(2)}) %all-to-all-start.7) | async-done | bytes 294944 | tf_op jit(solution)/shard_map/all_to_all | solution.py:110
  312.2 9.5 %all-to-all-start.4 = ((bf16[128,1,16,72]{3,2,1,0:T(8,128)(2,1)}), bf16[128,1,16,72]{3,2,1,0:T(8,128)(2,1)S(1)}, u32[]{:S(2)}, u32[]{:S(2)}) async-start(bf16[128,1,16,72]{3,2,1,0:T(8,128)(2,1)} %copy.77), calls=%async_computation.4 | async-start | bytes 1048576 | tf_op jit(solution)/shard_map/all_to_all | solution.py:110
  323.4 29.0 %all-to-all-done.4 = bf16[128,1,16,72]{3,2,1,0:T(8,128)(2,1)S(1)} async-done(((bf16[128,1,16,72]{3,2,1,0:T(8,128)(2,1)}), bf16[128,1,16,72]{3,2,1,0:T(8,128)(2,1)S(1)}, u32[]{:S(2)}, u32[]{:S(2)}) %all-to-all-start.4) | async-done | bytes 294944 | tf_op jit(solution)/shard_map/all_to_all | solution.py:110
  352.4 10.0 %all-to-all-start.5 = ((bf16[128,1,16,72]{3,2,1,0:T(8,128)(2,1)}), bf16[128,1,16,72]{3,2,1,0:T(8,128)(2,1)}, u32[]{:S(2)}, u32[]{:S(2)}) async-start(bf16[128,1,16,72]{3,2,1,0:T(8,128)(2,1)} %copy.80), calls=%async_computation.5 | async-start | bytes 1048576 | tf_op jit(solution)/shard_map/all_to_all | solution.py:110
  363.6 2.3 reshape.172
  365.9 2.2 copy.86
  368.1 2.3 squeeze_reshape.3
  371.5 2.3 reshape.168
  375.3 33.8 %psum.28 = f32[1152]{0:T(1024)S(1)} all-reduce(f32[1152]{0:T(1024)S(1)} %fusion.6), channel_id=1, replica_groups=mesh['clip'=4,'tx_0'=8,'tx_1'=2,'ty_0'=2,'ty_1'=4] {'tx_0'}, use_global_device_ids=true, to_apply=%region_4.0 | all-reduce | flops 1152 | bytes 9216 | tf_op jit(solution)/shard_map/psum | solution.py:24
  409.2 2.5 psum.29
  411.7 13.8 %psum.30 = f32[1152]{0:T(1024)S(1)} all-reduce(f32[1152]{0:T(1024)S(1)} %psum.29), channel_id=1, replica_groups=mesh['clip'=4,'tx_0'=8,'tx_1'=2,'ty_0'=2,'ty_1'=4] {'ty_0'}, use_global_device_ids=true, to_apply=%region_6.0 | all-reduce | flops 1152 | bytes 9216 | tf_op jit(solution)/shard_map/psum | solution.py:24
  425.4 11.1 %psum.31 = f32[1152]{0:T(1024)} all-reduce(f32[1152]{0:T(1024)S(1)} %psum.30), channel_id=1, replica_groups=mesh['clip'=4,'tx_0'=8,'tx_1'=2,'ty_0'=2,'ty_1'=4] {'ty_1'}, use_global_device_ids=true, to_apply=%region_7.0 | all-reduce | flops 1152 | bytes 9216 | tf_op jit(solution)/shard_map/psum | solution.py:24
  (49 shorter events, 29.7 us)
Async XLA Ops:
  7.2 23.6 %copy-start.5 = (bf16[1,128,1152]{2,1,0:T(8,128)(2,1)S(1)}, bf16[1,128,1152]{2,1,0:T(8,128)(2,1)}, u32[]{:S(2)}) copy-start(bf16[1,128,1152]{2,1,0:T(8,128)(2,1)} %param.7) | copy-start | bytes 884740
  7.2 137.2 %all-gather.2.cloned.1.call-start = ((), (), s32[]{:S(2)}) async-start(), calls=%async_computation.8 | async-start | bytes 2820096 | tf_op jit(solution)/shard_map/all_gather | solution.py:93
  9.8 134.6 %copy-start.4 = (bf16[1,128,1152]{2,1,0:T(8,128)(2,1)S(1)}, bf16[1,128,1152]{2,1,0:T(8,128)(2,1)}, u32[]{:S(2)}) copy-start(bf16[1,128,1152]{2,1,0:T(8,128)(2,1)} %param.9) | copy-start | bytes 884740
  9.8 134.6 %copy-start.8 = (f32[1152]{0:T(1024)S(1)}, f32[1152]{0:T(1024)}, u32[]{:S(2)}) copy-start(f32[1152]{0:T(1024)} %param.10) | copy-start | bytes 13828
  10.8 55.5 %all-to-all-start = ((bf16[1,128,16,72]{3,2,0,1:T(8,128)(2,1)}), bf16[1,128,16,72]{3,2,0,1:T(8,128)(2,1)S(1)}, u32[]{:S(2)}, u32[]{:S(2)}) async-start(bf16[1,128,16,72]{3,2,0,1:T(8,128)(2,1)} %bitcast.2), calls=%async_computation | async-start | bytes 1048576 | tf_op jit(solution)/shard_map/all_to_all | solution.py:102
  66.3 82.7 %all-to-all-start.1 = ((bf16[1,128,16,72]{3,2,0,1:T(8,128)(2,1)}), bf16[1,128,16,72]{3,2,0,1:T(8,128)(2,1)S(1)}, u32[]{:S(2)}, u32[]{:S(2)}) async-start(bf16[1,128,16,72]{3,2,0,1:T(8,128)(2,1)} %bitcast.6), calls=%async_computation.1 | async-start | bytes 1048576 | tf_op jit(solution)/shard_map/all_to_all | solution.py:102
  75.9 85.1 %copy-start.6 = (bf16[1,128,1152]{2,1,0:T(8,128)(2,1)S(1)}, bf16[1,128,1152]{2,1,0:T(8,128)(2,1)}, u32[]{:S(2)}) copy-start(bf16[1,128,1152]{2,1,0:T(8,128)(2,1)} %param.8) | copy-start | bytes 884740
  149.0 42.7 %all-to-all-start.2 = ((bf16[1,128,16,72]{3,2,0,1:T(8,128)(2,1)}), bf16[1,128,16,72]{3,2,0,1:T(8,128)(2,1)S(1)}, u32[]{:S(2)}, u32[]{:S(2)}) async-start(bf16[1,128,16,72]{3,2,0,1:T(8,128)(2,1)} %bitcast.11), calls=%async_computation.2 | async-start | bytes 1048576 | tf_op jit(solution)/shard_map/all_to_all | solution.py:102
  191.7 40.2 %all-to-all-start.3 = ((bf16[1,128,16,72]{3,2,0,1:T(8,128)(2,1)}), bf16[1,128,16,72]{3,2,0,1:T(8,128)(2,1)S(1)}, u32[]{:S(2)}, u32[]{:S(2)}) async-start(bf16[1,128,16,72]{3,2,0,1:T(8,128)(2,1)} %bitcast.15), calls=%async_computation.3 | async-start | bytes 1048576 | tf_op jit(solution)/shard_map/all_to_all | solution.py:102
  231.8 40.2 %all-to-all-start.6 = ((bf16[128,1,16,72]{3,2,1,0:T(8,128)(2,1)}), bf16[128,1,16,72]{3,2,1,0:T(8,128)(2,1)S(1)}, u32[]{:S(2)}, u32[]{:S(2)}) async-start(bf16[128,1,16,72]{3,2,1,0:T(8,128)(2,1)} %copy.83), calls=%async_computation.6 | async-start | bytes 1048576 | tf_op jit(solution)/shard_map/all_to_all | solution.py:110
  241.8 30.2 %copy-start.7 = (bf16[1,128,16,72]{1,3,2,0:T(8,128)(2,1)}, bf16[1,128,16,72]{1,3,2,0:T(8,128)(2,1)S(1)}, u32[]{:S(2)}) copy-start(bf16[1,128,16,72]{1,3,2,0:T(8,128)(2,1)S(1)} %copy.72) | copy-start | bytes 884740
  272.0 40.2 %all-to-all-start.7 = ((bf16[128,1,16,72]{3,2,1,0:T(8,128)(2,1)}), bf16[128,1,16,72]{3,2,1,0:T(8,128)(2,1)S(1)}, u32[]{:S(2)}, u32[]{:S(2)}) async-start(bf16[128,1,16,72]{3,2,1,0:T(8,128)(2,1)} %copy.85), calls=%async_computation.7 | async-start | bytes 1048576 | tf_op jit(solution)/shard_map/all_to_all | solution.py:110
  312.2 50.2 %copy-start.1 = (bf16[128,1,16,72]{3,2,1,0:T(8,128)(2,1)}, bf16[128,1,16,72]{3,2,1,0:T(8,128)(2,1)S(1)}, u32[]{:S(2)}) copy-start(bf16[128,1,16,72]{3,2,1,0:T(8,128)(2,1)S(1)} %all-to-all-done.7) | copy-start | bytes 884740
  312.2 40.2 %all-to-all-start.4 = ((bf16[128,1,16,72]{3,2,1,0:T(8,128)(2,1)}), bf16[128,1,16,72]{3,2,1,0:T(8,128)(2,1)S(1)}, u32[]{:S(2)}, u32[]{:S(2)}) async-start(bf16[128,1,16,72]{3,2,1,0:T(8,128)(2,1)} %copy.77), calls=%async_computation.4 | async-start | bytes 1048576 | tf_op jit(solution)/shard_map/all_to_all | solution.py:110
  352.4 10.1 %copy-start.2 = (bf16[128,1,16,72]{3,2,1,0:T(8,128)(2,1)}, bf16[128,1,16,72]{3,2,1,0:T(8,128)(2,1)S(1)}, u32[]{:S(2)}) copy-start(bf16[128,1,16,72]{3,2,1,0:T(8,128)(2,1)S(1)} %all-to-all-done.4) | copy-start | bytes 884740
  352.4 84.1 %all-to-all-start.5 = ((bf16[128,1,16,72]{3,2,1,0:T(8,128)(2,1)}), bf16[128,1,16,72]{3,2,1,0:T(8,128)(2,1)}, u32[]{:S(2)}, u32[]{:S(2)}) async-start(bf16[128,1,16,72]{3,2,1,0:T(8,128)(2,1)} %copy.80), calls=%async_computation.5 | async-start | bytes 1048576 | tf_op jit(solution)/shard_map/all_to_all | solution.py:110
  362.5 11.3 %copy-start = (bf16[1152,1152]{1,0:T(8,128)(2,1)S(1)}, bf16[1152,1152]{1,0:T(8,128)(2,1)}, u32[]{:S(2)}) copy-start(bf16[1152,1152]{1,0:T(8,128)(2,1)} %all-gather.2.cloned.1.call-done) | copy-start | bytes 7962628
  363.6 6.8 %copy-start.3 = (bf16[128,1,16,72]{3,2,1,0:T(8,128)(2,1)S(1)}, bf16[128,1,16,72]{3,2,1,0:T(8,128)(2,1)}, u32[]{:S(2)}) copy-start(bf16[128,1,16,72]{3,2,1,0:T(8,128)(2,1)} %copy-done.2) | copy-start | bytes 884740
Sparse Core Ops, SparseCore 0:
  10.1 134.2 all-gather.1
where the time goes:
time: 447 us; the launch traced here: 446 us
  waiting for transfers between devices  240 us (54%)
  starting transfers between devices  89.7 us (20%)
  blocking collectives  61.2 us (14%)
  local copies, waits for them, and re-layouts  29.1 us (7%)
  between operations  14.3 us (3%)
  matrix products  11.6 us (3%)
    all_to_all x4, waiting for transfers between devices, per_device(): lax.all_to_all(shortened(prepared), TX_TY, split_axis=1, concat_axis=0, t...  87.1 us
    all_to_all x4, waiting for transfers between devices, per_device(): lax.all_to_all(shortened(outgoing), TX_TY, split_axis=0, concat_axis=1, t...  83.8 us
    all_gather x1, waiting for transfers between devices, per_device(): full_weight = lax.all_gather(out_weight, TX, axis=0, tiled=True)  68.5 us
    psum x4, blocking collectives, over_axes(): x = lax.psum(x, axis)  61.2 us
    all_to_all x4, starting transfers between devices, per_device(): lax.all_to_all(shortened(prepared), TX_TY, split_axis=1, concat_axis=0, t...  51.2 us
    all_to_all x4, starting transfers between devices, per_device(): lax.all_to_all(shortened(outgoing), TX_TY, split_axis=0, concat_axis=1, t...  38.5 us
  transfers between devices with their start and end apart: 9, of which 7 were waited for; matrix products, arithmetic and copies ran while one was open for 9% of the time, Pallas kernels for 0%

commit v1 on v0

--- a/solution.py
+++ b/solution.py
@@ -21,7 +21,7 @@
 
 def over_axes(x, axes):
     for axis in axes:
-        x = lax.psum(x, axis)
+        x = jnp.sum(lax.all_gather(x, axis), axis=0)
     return x
 
 

time: 447 us -> 466 us (1.043)
  blocking collectives: 61.2 us -> 81.8 us
    all_gather x0 -> x4, blocking collectives: none -> 81.8 us  [over_axes(): x = jnp.sum(lax.all_gather(x, axis), axis=0)]
    psum x4 -> x0, blocking collectives: 61.2 us -> none  [over_axes(): x = lax.psum(x, axis)]
  transfers between devices with their start and end apart: 9 -> 9, of which waited for: 7 -> 7; matrix products, arithmetic and copies ran while one was open for 9% -> 8% of each run, Pallas kernels for 0% -> 0%
where the time goes in v1:
time: 466 us; the launch traced here: 465 us
  waiting for transfers between devices  240 us (52%)
  starting transfers between devices  90.3 us (19%)
  blocking collectives  81.8 us (18%)
  local copies, waits for them, and re-layouts  27.6 us (6%)
  between operations  14.3 us (3%)
  matrix products  9.93 us (2%)
    all_to_all x4, waiting for transfers between devices, per_device(): lax.all_to_all(shortened(prepared), TX_TY, split_axis=1, concat_axis=0, t...  89.3 us
    all_gather x4, blocking collectives, over_axes(): x = jnp.sum(lax.all_gather(x, axis), axis=0)  81.8 us
    all_to_all x4, waiting for transfers between devices, per_device(): lax.all_to_all(shortened(outgoing), TX_TY, split_axis=0, concat_axis=1, t...  81.7 us
    all_gather x1, waiting for transfers between devices, per_device(): full_weight = lax.all_gather(out_weight, TX, axis=0, tiled=True)  68.6 us
    all_to_all x4, starting transfers between devices, per_device(): lax.all_to_all(shortened(prepared), TX_TY, split_axis=1, concat_axis=0, t...  51.1 us
    all_to_all x4, starting transfers between devices, per_device(): lax.all_to_all(shortened(outgoing), TX_TY, split_axis=0, concat_axis=1, t...  39.1 us
  transfers between devices with their start and end apart: 9, of which 7 were waited for; matrix products, arithmetic and copies ran while one was open for 8% of the time, Pallas kernels for 0%

profile of v1, /device:TPU:6, one launch (start us, length us, event | category | flops | bytes accessed | tf_op | source)
XLA Modules:
  0.0 464.9 jit_solution(17225425946948875818)
XLA Ops:
  7.9 1.9 reshape_squeeze.9
  10.8 20.0 %all-to-all-start = ((bf16[1,128,16,72]{3,2,0,1:T(8,128)(2,1)}), bf16[1,128,16,72]{3,2,0,1:T(8,128)(2,1)S(1)}, u32[]{:S(2)}, u32[]{:S(2)}) async-start(bf16[1,128,16,72]{3,2,0,1:T(8,128)(2,1)} %bitcast.2), calls=%async_computation | async-start | bytes 1048576 | tf_op jit(solution)/shard_map/all_to_all | solution.py:102
  32.6 33.7 %all-to-all-done = bf16[1,128,16,72]{3,2,0,1:T(8,128)(2,1)S(1)} async-done(((bf16[1,128,16,72]{3,2,0,1:T(8,128)(2,1)}), bf16[1,128,16,72]{3,2,0,1:T(8,128)(2,1)S(1)}, u32[]{:S(2)}, u32[]{:S(2)}) %all-to-all-start) | async-done | bytes 294944 | tf_op jit(solution)/shard_map/all_to_all | solution.py:102
  66.3 9.5 %all-to-all-start.1 = ((bf16[1,128,16,72]{3,2,0,1:T(8,128)(2,1)}), bf16[1,128,16,72]{3,2,0,1:T(8,128)(2,1)S(1)}, u32[]{:S(2)}, u32[]{:S(2)}) async-start(bf16[1,128,16,72]{3,2,0,1:T(8,128)(2,1)} %bitcast.6), calls=%async_computation.1 | async-start | bytes 1048576 | tf_op jit(solution)/shard_map/all_to_all | solution.py:102
  75.9 68.6 %all-gather.10.cloned.1.call-done = bf16[1152,1152]{1,0:T(8,128)(2,1)} async-done(((bf16[72,1152]{1,0:T(8,128)(2,1)}), bf16[1152,1152]{1,0:T(8,128)(2,1)}) %all-gather.10.cloned.1.call-update) | async-done | bytes 2654224 | tf_op jit(solution)/shard_map/all_gather | solution.py:93
  144.5 2.7 convolution_convert_fusion
  149.1 12.0 %all-to-all-start.2 = ((bf16[1,128,16,72]{3,2,0,1:T(8,128)(2,1)}), bf16[1,128,16,72]{3,2,0,1:T(8,128)(2,1)S(1)}, u32[]{:S(2)}, u32[]{:S(2)}) async-start(bf16[1,128,16,72]{3,2,0,1:T(8,128)(2,1)} %bitcast.11), calls=%async_computation.2 | async-start | bytes 1048576 | tf_op jit(solution)/shard_map/all_to_all | solution.py:102
  162.9 28.8 %all-to-all-done.2 = bf16[1,128,16,72]{3,2,0,1:T(8,128)(2,1)S(1)} async-done(((bf16[1,128,16,72]{3,2,0,1:T(8,128)(2,1)}), bf16[1,128,16,72]{3,2,0,1:T(8,128)(2,1)S(1)}, u32[]{:S(2)}, u32[]{:S(2)}) %all-to-all-start.2) | async-done | bytes 294944 | tf_op jit(solution)/shard_map/all_to_all | solution.py:102
  191.7 9.7 %all-to-all-start.3 = ((bf16[1,128,16,72]{3,2,0,1:T(8,128)(2,1)}), bf16[1,128,16,72]{3,2,0,1:T(8,128)(2,1)S(1)}, u32[]{:S(2)}, u32[]{:S(2)}) async-start(bf16[1,128,16,72]{3,2,0,1:T(8,128)(2,1)} %bitcast.15), calls=%async_computation.3 | async-start | bytes 1048576 | tf_op jit(solution)/shard_map/all_to_all | solution.py:102
  205.1 26.9 %all-to-all-done.3 = bf16[1,128,16,72]{3,2,0,1:T(8,128)(2,1)S(1)} async-done(((bf16[1,128,16,72]{3,2,0,1:T(8,128)(2,1)}), bf16[1,128,16,72]{3,2,0,1:T(8,128)(2,1)S(1)}, u32[]{:S(2)}, u32[]{:S(2)}) %all-to-all-start.3) | async-done | bytes 294944 | tf_op jit(solution)/shard_map/all_to_all | solution.py:102
  231.9 9.5 %all-to-all-start.6 = ((bf16[128,1,16,72]{3,2,1,0:T(8,128)(2,1)}), bf16[128,1,16,72]{3,2,1,0:T(8,128)(2,1)S(1)}, u32[]{:S(2)}, u32[]{:S(2)}) async-start(bf16[128,1,16,72]{3,2,1,0:T(8,128)(2,1)} %copy.83), calls=%async_computation.6 | async-start | bytes 1048576 | tf_op jit(solution)/shard_map/all_to_all | solution.py:110
  244.7 27.5 %all-to-all-done.6 = bf16[128,1,16,72]{3,2,1,0:T(8,128)(2,1)S(1)} async-done(((bf16[128,1,16,72]{3,2,1,0:T(8,128)(2,1)}), bf16[128,1,16,72]{3,2,1,0:T(8,128)(2,1)S(1)}, u32[]{:S(2)}, u32[]{:S(2)}) %all-to-all-start.6) | async-done | bytes 294944 | tf_op jit(solution)/shard_map/all_to_all | solution.py:110
  272.1 9.5 %all-to-all-start.7 = ((bf16[128,1,16,72]{3,2,1,0:T(8,128)(2,1)}), bf16[128,1,16,72]{3,2,1,0:T(8,128)(2,1)S(1)}, u32[]{:S(2)}, u32[]{:S(2)}) async-start(bf16[128,1,16,72]{3,2,1,0:T(8,128)(2,1)} %copy.85), calls=%async_computation.7 | async-start | bytes 1048576 | tf_op jit(solution)/shard_map/all_to_all | solution.py:110
  281.6 1.6 fusion.5
  284.7 27.5 %all-to-all-done.7 = bf16[128,1,16,72]{3,2,1,0:T(8,128)(2,1)S(1)} async-done(((bf16[128,1,16,72]{3,2,1,0:T(8,128)(2,1)}), bf16[128,1,16,72]{3,2,1,0:T(8,128)(2,1)S(1)}, u32[]{:S(2)}, u32[]{:S(2)}) %all-to-all-start.7) | async-done | bytes 294944 | tf_op jit(solution)/shard_map/all_to_all | solution.py:110
  312.3 10.0 %all-to-all-start.4 = ((bf16[128,1,16,72]{3,2,1,0:T(8,128)(2,1)}), bf16[128,1,16,72]{3,2,1,0:T(8,128)(2,1)}, u32[]{:S(2)}, u32[]{:S(2)}) async-start(bf16[128,1,16,72]{3,2,1,0:T(8,128)(2,1)} %copy.77), calls=%async_computation.4 | async-start | bytes 1048576 | tf_op jit(solution)/shard_map/all_to_all | solution.py:110
  323.6 2.3 copy.80
  325.9 26.7 %all-to-all-done.4 = bf16[128,1,16,72]{3,2,1,0:T(8,128)(2,1)} async-done(((bf16[128,1,16,72]{3,2,1,0:T(8,128)(2,1)}), bf16[128,1,16,72]{3,2,1,0:T(8,128)(2,1)}, u32[]{:S(2)}, u32[]{:S(2)}) %all-to-all-start.4) | async-done | bytes 294944 | tf_op jit(solution)/shard_map/all_to_all | solution.py:110
  352.6 10.0 %all-to-all-start.5 = ((bf16[128,1,16,72]{3,2,1,0:T(8,128)(2,1)}), bf16[128,1,16,72]{3,2,1,0:T(8,128)(2,1)}, u32[]{:S(2)}, u32[]{:S(2)}) async-start(bf16[128,1,16,72]{3,2,1,0:T(8,128)(2,1)} %copy.80), calls=%async_computation.5 | async-start | bytes 1048576 | tf_op jit(solution)/shard_map/all_to_all | solution.py:110
  363.8 2.3 reshape.172
  370.2 54.5 %all-gather.4 = f32[8,1,1152]{2,1,0:T(1,128)S(1)} all-gather(f32[1,1,1152]{2,1,0:T(1,128)S(1)} %reshape.180), channel_id=2, replica_groups=mesh['clip'=4,'tx_0'=8,'tx_1'=2,'ty_0'=2,'ty_1'=4] {'tx_0'}, dimensions={0}, use_global_device_ids=true | all-gather | bytes 41472 | tf_op jit(solution)/shard_map/all_gather | solution.py:24
  424.8 1.8 all-gather.5
  426.6 13.1 %all-gather.6 = f32[2,1,1152]{2,1,0:T(1,128)S(1)} all-gather(f32[1,1,1152]{2,1,0:T(1,128)S(1)} %reshape.184), channel_id=4, replica_groups=mesh['clip'=4,'tx_0'=8,'tx_1'=2,'ty_0'=2,'ty_1'=4] {'ty_0'}, dimensions={0}, use_global_device_ids=true | all-gather | bytes 13824 | tf_op jit(solution)/shard_map/all_gather | solution.py:24
  439.7 12.5 %all-gather.7 = f32[4,1,1152]{2,1,0:T(1,128)S(1)} all-gather(f32[1,1,1152]{2,1,0:T(1,128)S(1)} %reshape.186), channel_id=5, replica_groups=mesh['clip'=4,'tx_0'=8,'tx_1'=2,'ty_0'=2,'ty_1'=4] {'ty_1'}, dimensions={0}, use_global_device_ids=true | all-gather | bytes 23040 | tf_op jit(solution)/shard_map/all_gather | solution.py:24
  (53 shorter events, 28.2 us)
Async XLA Ops:
  7.2 23.6 %copy-start.3 = (bf16[1,128,1152]{2,1,0:T(8,128)(2,1)S(1)}, bf16[1,128,1152]{2,1,0:T(8,128)(2,1)}, u32[]{:S(2)}) copy-start(bf16[1,128,1152]{2,1,0:T(8,128)(2,1)} %param.7) | copy-start | bytes 884740
  7.2 137.3 %all-gather.10.cloned.1.call-start = ((), (), s32[]{:S(2)}) async-start(), calls=%async_computation.8 | async-start | bytes 2820096 | tf_op jit(solution)/shard_map/all_gather | solution.py:93
  9.8 134.7 %copy-start.2 = (bf16[1,128,1152]{2,1,0:T(8,128)(2,1)S(1)}, bf16[1,128,1152]{2,1,0:T(8,128)(2,1)}, u32[]{:S(2)}) copy-start(bf16[1,128,1152]{2,1,0:T(8,128)(2,1)} %param.9) | copy-start | bytes 884740
  9.8 134.7 %copy-start.5 = (f32[1152]{0:T(1024)S(1)}, f32[1152]{0:T(1024)}, u32[]{:S(2)}) copy-start(f32[1152]{0:T(1024)} %param.10) | copy-start | bytes 13828
  10.8 55.5 %all-to-all-start = ((bf16[1,128,16,72]{3,2,0,1:T(8,128)(2,1)}), bf16[1,128,16,72]{3,2,0,1:T(8,128)(2,1)S(1)}, u32[]{:S(2)}, u32[]{:S(2)}) async-start(bf16[1,128,16,72]{3,2,0,1:T(8,128)(2,1)} %bitcast.2), calls=%async_computation | async-start | bytes 1048576 | tf_op jit(solution)/shard_map/all_to_all | solution.py:102
  66.3 82.7 %all-to-all-start.1 = ((bf16[1,128,16,72]{3,2,0,1:T(8,128)(2,1)}), bf16[1,128,16,72]{3,2,0,1:T(8,128)(2,1)S(1)}, u32[]{:S(2)}, u32[]{:S(2)}) async-start(bf16[1,128,16,72]{3,2,0,1:T(8,128)(2,1)} %bitcast.6), calls=%async_computation.1 | async-start | bytes 1048576 | tf_op jit(solution)/shard_map/all_to_all | solution.py:102
  75.9 85.2 %copy-start.4 = (bf16[1,128,1152]{2,1,0:T(8,128)(2,1)S(1)}, bf16[1,128,1152]{2,1,0:T(8,128)(2,1)}, u32[]{:S(2)}) copy-start(bf16[1,128,1152]{2,1,0:T(8,128)(2,1)} %param.8) | copy-start | bytes 884740
  149.1 42.7 %all-to-all-start.2 = ((bf16[1,128,16,72]{3,2,0,1:T(8,128)(2,1)}), bf16[1,128,16,72]{3,2,0,1:T(8,128)(2,1)S(1)}, u32[]{:S(2)}, u32[]{:S(2)}) async-start(bf16[1,128,16,72]{3,2,0,1:T(8,128)(2,1)} %bitcast.11), calls=%async_computation.2 | async-start | bytes 1048576 | tf_op jit(solution)/shard_map/all_to_all | solution.py:102
  191.7 40.2 %all-to-all-start.3 = ((bf16[1,128,16,72]{3,2,0,1:T(8,128)(2,1)}), bf16[1,128,16,72]{3,2,0,1:T(8,128)(2,1)S(1)}, u32[]{:S(2)}, u32[]{:S(2)}) async-start(bf16[1,128,16,72]{3,2,0,1:T(8,128)(2,1)} %bitcast.15), calls=%async_computation.3 | async-start | bytes 1048576 | tf_op jit(solution)/shard_map/all_to_all | solution.py:102
  202.9 2.2 copy-start.6
  231.9 40.2 %all-to-all-start.6 = ((bf16[128,1,16,72]{3,2,1,0:T(8,128)(2,1)}), bf16[128,1,16,72]{3,2,1,0:T(8,128)(2,1)S(1)}, u32[]{:S(2)}, u32[]{:S(2)}) async-start(bf16[128,1,16,72]{3,2,1,0:T(8,128)(2,1)} %copy.83), calls=%async_computation.6 | async-start | bytes 1048576 | tf_op jit(solution)/shard_map/all_to_all | solution.py:110
  272.1 40.2 %all-to-all-start.7 = ((bf16[128,1,16,72]{3,2,1,0:T(8,128)(2,1)}), bf16[128,1,16,72]{3,2,1,0:T(8,128)(2,1)S(1)}, u32[]{:S(2)}, u32[]{:S(2)}) async-start(bf16[128,1,16,72]{3,2,1,0:T(8,128)(2,1)} %copy.85), calls=%async_computation.7 | async-start | bytes 1048576 | tf_op jit(solution)/shard_map/all_to_all | solution.py:110
  312.3 10.0 %copy-start.1 = (bf16[128,1,16,72]{3,2,1,0:T(8,128)(2,1)}, bf16[128,1,16,72]{3,2,1,0:T(8,128)(2,1)S(1)}, u32[]{:S(2)}) copy-start(bf16[128,1,16,72]{3,2,1,0:T(8,128)(2,1)S(1)} %all-to-all-done.7) | copy-start | bytes 884740
  312.3 40.3 %all-to-all-start.4 = ((bf16[128,1,16,72]{3,2,1,0:T(8,128)(2,1)}), bf16[128,1,16,72]{3,2,1,0:T(8,128)(2,1)}, u32[]{:S(2)}, u32[]{:S(2)}) async-start(bf16[128,1,16,72]{3,2,1,0:T(8,128)(2,1)} %copy.77), calls=%async_computation.4 | async-start | bytes 1048576 | tf_op jit(solution)/shard_map/all_to_all | solution.py:110
  323.6 45.1 %copy-start = (bf16[1152,1152]{1,0:T(8,128)(2,1)S(1)}, bf16[1152,1152]{1,0:T(8,128)(2,1)}, u32[]{:S(2)}) copy-start(bf16[1152,1152]{1,0:T(8,128)(2,1)} %all-gather.10.cloned.1.call-done) | copy-start | bytes 7962628
  352.6 102.8 %all-to-all-start.5 = ((bf16[128,1,16,72]{3,2,1,0:T(8,128)(2,1)}), bf16[128,1,16,72]{3,2,1,0:T(8,128)(2,1)}, u32[]{:S(2)}, u32[]{:S(2)}) async-start(bf16[128,1,16,72]{3,2,1,0:T(8,128)(2,1)} %copy.80), calls=%async_computation.5 | async-start | bytes 1048576 | tf_op jit(solution)/shard_map/all_to_all | solution.py:110
Sparse Core Ops, SparseCore 0:
  10.1 134.3 all-gather.9
